TPU v7x, 32 devices: a whole 2x2x4 slice. The times are simulated.
32 devices in a mesh: mem: 8 (over z, y), band: 4 (over x, core).
Axes of the slice: x: 2, y: 2, z: 4, core: 2. Of those that a mesh axis runs over, the one named last changes fastest.
Arguments:
- alpha: bfloat16 [16, 4, 320, 720], P('mem', None, 'band'), may hold values from -6 to 6
- static_ctl: bfloat16 [4, 320, 720], P(None, 'band'), may hold values from -6 to 6
- perturbations: bfloat16 [16, 4, 320, 720], P('mem', None, None, 'band'), may hold values from -6 to 6
- static_std: float32 [4, 320, 720], P(None, None, 'band'), may hold values from 0.5 to 2
- lon_root: bfloat16 [720, 720], replicated, may hold values from -0.11 to 1.11
- lat_root: bfloat16 [320, 320], replicated, may hold values from -0.11 to 1.11
- jacobian: bfloat16 [32, 4, 320, 720], P(None, None, 'mem', 'band'), may hold values from -3 to 3
- obs_count: int32 [320, 720], P('mem', 'band'), may hold values from 1 to 6
- channel_mask: int32 [32, 320, 720], P(None, 'mem', 'band'), may hold values 0 or 1
- channel_error: float32 [32], replicated, may hold values from 1 to 2
- member_weight: int32 [16], replicated, may hold values from 1 to 4
Outputs:
- grad_alpha: float32 [16, 4, 320, 720], P('mem', None, 'band')
- grad_static: float32 [4, 320, 720], P(None, 'band')
All inputs are finite; a program needn't handle non-finite values. No bound on the sum of `channel_mask` on one device may be relied on, other than what follows from the above.
Results may differ from a plain program's by a relative error of at most 0.0055.
Values may be sent and summed in bfloat16 or wider, within the bound.
No kernel may reach another device: no remote copies, remote signals or barrier semaphores. Data moves between devices by JAX's collectives and lax.ppermute only.
A program may use at most 64 MiB of HBM per device.

v0:
```python
import jax
import jax.numpy as jnp
from jax import lax
from jax.sharding import PartitionSpec as P


def shards(
    alpha,
    static_ctl,
    perturbations,
    static_std,
    lon_root,
    lat_root,
    jacobian,
    obs_count,
    channel_mask,
    channel_error,
    member_weight,
):
    members = alpha.shape[0]
    rows = jacobian.shape[2]
    rank = lax.axis_index("mem")
    weights = member_weight.astype(jnp.float32)
    coef = weights / jnp.sqrt(jnp.sum(weights * weights))
    own_coef = lax.dynamic_slice_in_dim(coef, rank * members, members, 0)
    fields = jnp.concatenate([alpha, static_ctl[None]], axis=0)
    along_lon = jnp.dot(fields, lon_root, preferred_element_type=jnp.float32).astype(jnp.bfloat16)
    regrouped = lax.all_to_all(along_lon, "band", split_axis=3, concat_axis=2, tiled=True)
    member_lat = jnp.einsum(
        "ij,msjk->msik", lat_root, regrouped[:members], preferred_element_type=jnp.float32
    )
    own_root = lax.dynamic_slice_in_dim(lat_root, rank * rows, rows, 0)
    own_static = jnp.einsum(
        "ij,sjk->sik", own_root, regrouped[members], preferred_element_type=jnp.float32
    )
    scaled = 0.8 * own_coef
    ensemble_term = jnp.sum(
        scaled[:, None, None, None] * perturbations.astype(jnp.float32) * member_lat, axis=0
    )
    summed = lax.psum(ensemble_term, "mem")
    own_sum = lax.dynamic_slice_in_dim(summed, rank * rows, rows, 1)
    own_std = lax.dynamic_slice_in_dim(static_std, rank * rows, rows, 1)
    increment = own_sum + 0.6 * own_std * own_static
    obs_weight = (
        channel_mask.astype(jnp.float32)
        * obs_count.astype(jnp.float32)[None]
        / (channel_error * channel_error)[:, None, None]
    )
    jac_full = jacobian.astype(jnp.float32)
    radiance = jnp.sum(jac_full * increment[None], axis=1)
    obs_gradient = jnp.sum(jac_full * (obs_weight * radiance)[:, None], axis=0).astype(jnp.bfloat16)
    band_gradient = lax.all_gather(obs_gradient, "mem", axis=1, tiled=True).astype(jnp.float32)
    member_adjoint = (
        scaled[:, None, None, None] * perturbations.astype(jnp.float32) * band_gradient[None]
    ).astype(jnp.bfloat16)
    static_adjoint = (0.6 * static_std * band_gradient).astype(jnp.bfloat16)
    adjoints = jnp.concatenate([member_adjoint, static_adjoint[None]], axis=0)
    back_lat = jnp.einsum(
        "ji,msjk->msik", lat_root, adjoints, preferred_element_type=jnp.float32
    ).astype(jnp.bfloat16)
    returned = lax.all_to_all(back_lat, "band", split_axis=2, concat_axis=3, tiled=True)
    back_lon = jnp.einsum("msil,jl->msij", returned, lon_root, preferred_element_type=jnp.float32)
    grad_alpha = alpha.astype(jnp.float32) + back_lon[:members]
    grad_static = static_ctl.astype(jnp.float32) + back_lon[members]
    return (grad_alpha, grad_static)


def solution(mesh):
    in_specs = (
        P("mem", None, "band", None),
        P(None, "band", None),
        P("mem", None, None, "band"),
        P(None, None, "band"),
        P(),
        P(),
        P(None, None, "mem", "band"),
        P("mem", "band"),
        P(None, "mem", "band"),
        P(),
        P(),
    )
    out_specs = (P("mem", None, "band", None), P(None, "band", None))
    return jax.shard_map(shards, mesh=mesh, in_specs=in_specs, out_specs=out_specs, check_vma=False)
```

profile of v0, /device:TPU:0, one launch (start us, length us, event | category | flops | bytes accessed | tf_op | source)
XLA Modules:
  0.0 232.6 jit_solution(4130602733582369304)
XLA Ops:
  7.2 1.2 copy-done
  8.4 2.7 %convolution_convert_fusion.1 = bf16[3,4,80,720]{3,2,1,0:T(8,128)(2,1)S(1)} fusion(bf16[1,4,80,720]{3,2,1,0:T(8,128)(2,1)} %bitcast.52, bf16[2,4,80,720]{3,2,1,0:T(8,128)(2,1)} %param.11, bf16[720,720]{1,0:T(8,128)(2,1)S(1)} %copy-done), kind=kOutput, calls=%fused_computation.13 | convolution fusion | flops 996710400 | bytes 3801600 | tf_op jit(solution)/shard_map/dot_general | solution.py:27
  11.1 3.3 %copy.28 = bf16[3,4,80,720]{2,1,0,3:T(4,128)(2,1)} copy(bf16[3,4,80,720]{3,2,1,0:T(8,128)(2,1)S(1)} %convolution_convert_fusion.1) | data formatting | bytes 2764800 | tf_op jit(solution)/shard_map/convert_element_type | solution.py:27
  14.4 4.4 %all-to-all-start = ((bf16[3,4,80,720]{2,1,0,3:T(4,128)(2,1)}), bf16[3,4,80,720]{2,1,0,3:T(4,128)(2,1)S(1)}, u32[]{:S(2)}, u32[]{:S(2)}) async-start(bf16[3,4,80,720]{2,1,0,3:T(4,128)(2,1)} %copy.28), calls=%async_computation | async-start | bytes 4423680 | tf_op jit(solution)/shard_map/all_to_all | solution.py:28
  18.7 0.6 multiply_reduce_fusion
  20.1 25.5 %all-to-all-done = bf16[3,4,80,720]{2,1,0,3:T(4,128)(2,1)S(1)} async-done(((bf16[3,4,80,720]{2,1,0,3:T(4,128)(2,1)}), bf16[3,4,80,720]{2,1,0,3:T(4,128)(2,1)S(1)}, u32[]{:S(2)}, u32[]{:S(2)}) %all-to-all-start) | async-done | bytes 1382432 | tf_op jit(solution)/shard_map/all_to_all | solution.py:28
  45.6 3.8 %copy.29 = bf16[3,4,80,4,180]{4,2,3,1,0:T(8,128)(2,1)} copy(bf16[3,4,80,4,180]{2,1,0,4,3:T(4,128)(2,1)S(1)} %bitcast.46) | data formatting | bytes 2764800 | tf_op jit(solution)/shard_map/all_to_all | solution.py:28
  49.4 1.5 slice.21
  51.1 1.4 fusion.2
  52.5 1.5 copy.31
  54.1 0.3 constant_dynamic-slice_fusion
  54.6 1.1 slice.22
  55.7 83.2 %all-reduce.2.cloned.1.call-done = f32[4,320,180]{2,1,0:T(8,128)} async-done(((f32[4,320,180]{2,1,0:T(8,128)}), f32[4,320,180]{2,1,0:T(8,128)}) %all-reduce.2.cloned.1.call-update) | async-done | bytes 921616 | tf_op jit(solution)/shard_map/psum | solution.py:40
  138.9 1.2 fusion.13
  140.1 2.6 %fusion = f32[32,40,180]{2,1,0:T(8,128)S(1)} fusion(bf16[32,4,40,180]{3,2,1,0:T(8,128)(2,1)} %param.17, f32[4,40,180]{2,1,0:T(8,128)S(1)} %fusion.13), kind=kLoop, calls=%fused_computation.2 | loop fusion | flops 2534400 | bytes 2880000 | tf_op jit(solution)/shard_map/reduce_sum | solution.py:50
  143.0 1.5 copy-done.1
  144.5 0.7 fusion.1
  145.2 31.8 %all_gather.3 = bf16[4,320,180]{2,0,1:T(4,128)(2,1)S(1)} all-gather(bf16[4,40,180]{2,0,1:T(4,128)(2,1)S(1)} %copy.34), channel_id=1, replica_groups=mesh['mem'=8,'band'=4] {'mem'}, dimensions={1}, use_global_device_ids=true | all-gather | bytes 518400 | tf_op jit(solution)/shard_map/all_gather | solution.py:52
  177.0 0.9 copy.35
  178.1 1.0 copy-done.5
  179.1 0.4 multiply_convert_fusion
  179.5 0.6 copy-done.10
  180.0 2.5 %fusion.6 = bf16[3,4,320,180]{2,3,1,0:T(8,128)(2,1)} fusion(bf16[1,4,320,180]{2,3,1,0:T(8,128)(2,1)S(1)} %fusion.20, bf16[2,4,320,180]{2,3,1,0:T(8,128)(2,1)S(1)} %multiply_convert_fusion, bf16[320,320]{1,0:T(8,128)(2,1)S(1)} %copy-done.10), kind=kOutput, calls=%fused_computation.14 | convolution fusion | flops 443750400 | bytes 2969600 | tf_op jit(solution)/shard_map/ji,msjk->msik/dot_general | solution.py:58
  182.6 6.7 %copy.37 = bf16[3,4,320,180]{3,1,0,2:T(4,128)(2,1)S(1)} copy(bf16[3,4,320,180]{2,3,1,0:T(8,128)(2,1)} %fusion.6) | data formatting | bytes 2764800 | tf_op jit(solution)/shard_map/convert_element_type | solution.py:60
  189.2 26.8 %all_to_all.33 = bf16[3,4,320,180]{3,1,0,2:T(4,128)(2,1)S(1)} all-to-all(bf16[3,4,320,180]{3,1,0,2:T(4,128)(2,1)S(1)} %copy.37), channel_id=1, replica_groups=mesh['mem'=8,'band'=4] {'band'}, dimensions={2} | all-to-all | bytes 2764800 | tf_op jit(solution)/shard_map/all_to_all | solution.py:61
  216.0 0.3 copy.38
  216.3 1.0 copy.39
  217.4 2.5 %all_to_all.30 = bf16[3,4,80,720]{3,2,1,0:T(8,128)(2,1)} reshape(bf16[3,4,80,4,180]{4,3,2,1,0:T(4,128)(2,1)S(1)} %copy.39) | data formatting | bytes 2764800 | tf_op jit(solution)/shard_map/all_to_all | solution.py:61
  219.9 2.8 %fusion.16 = f32[3,4,80,720]{3,2,1,0:T(8,128)S(1)} fusion(bf16[3,4,80,720]{3,2,1,0:T(8,128)(2,1)} %all_to_all.30, bf16[720,720]{1,0:T(8,128)(2,1)S(1)} %copy-done), kind=kOutput, calls=%fused_computation.25 | convolution fusion | flops 995328000 | bytes 5184000 | tf_op jit(solution)/shard_map/msil,jl->msij/dot_general | solution.py:62
  222.7 1.0 fusion.19
  223.7 0.5 copy-done.6
  224.2 1.5 slice_add_fusion
  (32 shorter events, 1.1 us)
Async XLA Ops:
  7.2 1.3 copy-start
  14.4 4.4 %copy-start.11 = (s32[16]{0:T(128)S(1)}, s32[16]{0:T(128)}, u32[]{:S(2)}) copy-start(s32[16]{0:T(128)} %param.21) | copy-start | bytes 196
  14.4 31.3 %all-to-all-start = ((bf16[3,4,80,720]{2,1,0,3:T(4,128)(2,1)}), bf16[3,4,80,720]{2,1,0,3:T(4,128)(2,1)S(1)}, u32[]{:S(2)}, u32[]{:S(2)}) async-start(bf16[3,4,80,720]{2,1,0,3:T(4,128)(2,1)} %copy.28), calls=%async_computation | async-start | bytes 4423680 | tf_op jit(solution)/shard_map/all_to_all | solution.py:28
  18.7 120.2 %all-reduce.2.cloned.1.call-start = ((), (), s32[]{:S(2)}) async-start(), calls=%async_computation.2 | async-start | bytes 2621440 | tf_op jit(solution)/shard_map/psum | solution.py:40
  49.4 1.6 copy-start.4
  49.4 1.7 copy-start.9
  52.4 1.6 copy-start.12
  52.4 1.6 copy-start.8
  52.5 1.6 copy-start.2
  140.1 2.7 %copy-start.3 = (s32[32,40,180]{2,1,0:T(8,128)S(1)}, s32[32,40,180]{2,1,0:T(8,128)}, u32[]{:S(2)}) copy-start(s32[32,40,180]{2,1,0:T(8,128)} %param.19) | copy-start | bytes 2764804
  142.8 1.7 copy-start.1
  177.8 1.2 copy-start.5
  179.1 0.9 copy-start.10
  219.9 2.8 %copy-start.7 = (bf16[4,80,720]{2,1,0:T(8,128)(2,1)S(1)}, bf16[4,80,720]{2,1,0:T(8,128)(2,1)}, u32[]{:S(2)}) copy-start(bf16[4,80,720]{2,1,0:T(8,128)(2,1)} %param.12) | copy-start | bytes 1382404
  222.7 1.6 copy-start.6
Sparse Core Ops, SparseCore 0:
  54.1 84.7 all-reduce.1
where the time goes:
time: 233 us
  waiting for transfers between devices  109 us (47%)
  blocking collectives  58.6 us (25%)
  local copies, waits for them, and re-layouts  28 us (12%)
  between operations  15 us (6%)
  matrix products  10.5 us (5%)
  other arithmetic  7.4 us (3%)
  starting transfers between devices  4.37 us (2%)
    psum x1, waiting for transfers between devices, shards(): summed = lax.psum(ensemble_term, 'mem')  83.2 us
    all_gather x1, blocking collectives, shards(): lax.all_gather(obs_gradient, 'mem', axis=1, tiled=True).astype(jnp.float32)  31.8 us
    all_to_all x1, blocking collectives, shards(): lax.all_to_all(back_lat, 'band', split_axis=2, concat_axis=3, tiled=True)  26.8 us
    all_to_all x1, waiting for transfers between devices, shards(): lax.all_to_all(along_lon, 'band', split_axis=3, concat_axis=2, tiled=True)  25.5 us
    convert_element_type x1, local copies, waits for them, and re-layouts, shards(): back_lat = jnp.einsum('ji,msjk->msik', lat_root, adjoints, preferred_elem...  6.66 us
    unnamed x27, local copies, waits for them, and re-layouts  5.19 us
  transfers between devices with their start and end apart: 2, of which 2 were waited for; matrix products, arithmetic and copies ran while one was open for 1% of the time, Pallas kernels for 0%

commit v1 on v0

--- a/solution.py
+++ b/solution.py
@@ -2,6 +2,7 @@
 import jax.numpy as jnp
 from jax import lax
 from jax.sharding import PartitionSpec as P
+from jax.lax import axis_size, ppermute
 
 
 def shards(
@@ -37,7 +38,19 @@
     ensemble_term = jnp.sum(
         scaled[:, None, None, None] * perturbations.astype(jnp.float32) * member_lat, axis=0
     )
-    summed = lax.psum(ensemble_term, "mem")
+
+    def proceed_words(vec):
+        wide_n = axis_size("mem")
+        arr_next, main = (vec, 0)
+        while 1 << main < wide_n:
+            base_arr = ppermute(
+                arr_next, "mem", perm=[(it, it ^ 1 << main) for it in range(wide_n)]
+            )
+            arr_next = arr_next + base_arr
+            main = main + 1
+        return arr_next
+
+    summed = proceed_words(ensemble_term)
     own_sum = lax.dynamic_slice_in_dim(summed, rank * rows, rows, 1)
     own_std = lax.dynamic_slice_in_dim(static_std, rank * rows, rows, 1)
     increment = own_sum + 0.6 * own_std * own_static

time: 233 us -> 254 us (1.090)
  local copies, waits for them, and re-layouts: 28 us -> 41.6 us
  between operations: 15 us -> 1.52 us
  waiting for transfers between devices: 109 us -> 118 us
  starting transfers between devices: 4.37 us -> 11 us
  other arithmetic: 7.4 us -> 12 us
    ppermute x0 -> x3, waiting for transfers between devices: none -> 92 us  [proceed_words(): ppermute(arr_next, 'mem', perm=[(it, it ^ 1 << main) for it in range(wide...]
    psum x1 -> x0, waiting for transfers between devices: 83.2 us -> none  [shards(): summed = lax.psum(ensemble_term, 'mem')]
    ppermute x0 -> x3, starting transfers between devices: none -> 6.67 us  [proceed_words(): ppermute(arr_next, 'mem', perm=[(it, it ^ 1 << main) for it in range(wide...]
    add x0 -> x2, other arithmetic: none -> 4.6 us  [proceed_words(): arr_next = arr_next + base_arr]
    ppermute x0 -> x2, local copies, waits for them, and re-layouts: none -> 4.22 us  [proceed_words(): ppermute(arr_next, 'mem', perm=[(it, it ^ 1 << main) for it in range(wide...]
    add x0 -> x2, local copies, waits for them, and re-layouts: none -> 4.07 us  [proceed_words(): arr_next = arr_next + base_arr]
    unnamed x27 -> x28, local copies, waits for them, and re-layouts: 5.19 us -> 7.19 us
  transfers between devices with their start and end apart: 2 -> 4, of which waited for: 2 -> 4; matrix products, arithmetic and copies ran while one was open for 1% -> 1% of each run, Pallas kernels for 0% -> 0%
where the time goes in v1:
time: 254 us; the launch traced here: 253 us
  waiting for transfers between devices  118 us (46%)
  blocking collectives  58.4 us (23%)
  local copies, waits for them, and re-layouts  41.6 us (16%)
  other arithmetic  12 us (5%)
  starting transfers between devices  11 us (4%)
  matrix products  10.6 us (4%)
    ppermute x3, waiting for transfers between devices, proceed_words(): ppermute(arr_next, 'mem', perm=[(it, it ^ 1 << main) for it in range(wide...  92 us
    all_gather x1, blocking collectives, shards(): lax.all_gather(obs_gradient, 'mem', axis=1, tiled=True).astype(jnp.float32)  31.6 us
    all_to_all x1, blocking collectives, shards(): lax.all_to_all(back_lat, 'band', split_axis=2, concat_axis=3, tiled=True)  26.8 us
    all_to_all x1, waiting for transfers between devices, shards(): lax.all_to_all(along_lon, 'band', split_axis=3, concat_axis=2, tiled=True)  25.5 us
    unnamed x28, local copies, waits for them, and re-layouts  7.19 us
    ppermute x3, starting transfers between devices, proceed_words(): ppermute(arr_next, 'mem', perm=[(it, it ^ 1 << main) for it in range(wide...  6.67 us
    convert_element_type x1, local copies, waits for them, and re-layouts, shards(): back_lat = jnp.einsum('ji,msjk->msik', lat_root, adjoints, preferred_elem...  6.66 us
  transfers between devices with their start and end apart: 4, of which 4 were waited for; matrix products, arithmetic and copies ran while one was open for 1% of the time, Pallas kernels for 0%

profile of v1, /device:TPU:0, one launch (start us, length us, event | category | flops | bytes accessed | tf_op | source)
XLA Modules:
  0.0 252.7 jit_solution(177409859315027814)
XLA Ops:
  1.9 2.7 %convolution_convert_fusion.1 = bf16[3,4,80,720]{3,2,1,0:T(8,128)(2,1)S(1)} fusion(bf16[1,4,80,720]{3,2,1,0:T(8,128)(2,1)} %bitcast.54, bf16[2,4,80,720]{3,2,1,0:T(8,128)(2,1)} %param.11, bf16[720,720]{1,0:T(8,128)(2,1)S(1)} %copy-done), kind=kOutput, calls=%fused_computation.13 | convolution fusion | flops 996710400 | bytes 3801600 | tf_op jit(solution)/shard_map/dot_general | solution.py:28
  4.6 3.2 %copy.28 = bf16[3,4,80,720]{2,1,0,3:T(4,128)(2,1)} copy(bf16[3,4,80,720]{3,2,1,0:T(8,128)(2,1)S(1)} %convolution_convert_fusion.1) | data formatting | bytes 2764800 | tf_op jit(solution)/shard_map/convert_element_type | solution.py:28
  7.8 4.4 %all-to-all-start = ((bf16[3,4,80,720]{2,1,0,3:T(4,128)(2,1)}), bf16[3,4,80,720]{2,1,0,3:T(4,128)(2,1)S(1)}, u32[]{:S(2)}, u32[]{:S(2)}) async-start(bf16[3,4,80,720]{2,1,0,3:T(4,128)(2,1)} %copy.28), calls=%async_computation | async-start | bytes 4423680 | tf_op jit(solution)/shard_map/all_to_all | solution.py:29
  13.6 25.5 %all-to-all-done = bf16[3,4,80,720]{2,1,0,3:T(4,128)(2,1)S(1)} async-done(((bf16[3,4,80,720]{2,1,0,3:T(4,128)(2,1)}), bf16[3,4,80,720]{2,1,0,3:T(4,128)(2,1)S(1)}, u32[]{:S(2)}, u32[]{:S(2)}) %all-to-all-start) | async-done | bytes 1382432 | tf_op jit(solution)/shard_map/all_to_all | solution.py:29
  39.1 3.8 %copy.29 = bf16[3,4,80,4,180]{4,2,3,1,0:T(8,128)(2,1)} copy(bf16[3,4,80,4,180]{2,1,0,4,3:T(4,128)(2,1)S(1)} %bitcast.48) | data formatting | bytes 2764800 | tf_op jit(solution)/shard_map/all_to_all | solution.py:29
  42.8 1.5 slice.21
  44.5 1.4 fusion.2
  45.9 1.3 copy.31
  47.2 2.3 collective-permute-start
  49.5 1.5 copy.32
  51.0 22.8 %collective-permute-done = f32[4,320,180]{1,0,2:T(4,128)S(1)} collective-permute-done((f32[4,320,180]{1,0,2:T(4,128)}, f32[4,320,180]{1,0,2:T(4,128)S(1)}, u32[]{:S(2)}, u32[]{:S(2)}) %collective-permute-start) | collective-permute-done | bytes 921632 | tf_op jit(solution)/shard_map/ppermute | solution.py:46
  73.8 2.1 copy.33
  75.9 1.9 add.27
  77.8 1.6 copy.34
  79.4 1.8 collective-permute-start.1
  81.2 23.7 %collective-permute-done.1 = f32[4,320,180]{1,0,2:T(4,128)S(1)} collective-permute-done((f32[4,320,180]{1,0,2:T(4,128)}, f32[4,320,180]{1,0,2:T(4,128)S(1)}, u32[]{:S(2)}, u32[]{:S(2)}) %collective-permute-start.1) | collective-permute-done | bytes 921632 | tf_op jit(solution)/shard_map/ppermute | solution.py:46
  104.9 2.1 copy.35
  107.0 2.7 %add.28 = f32[4,320,180]{2,1,0:T(8,128)} add(f32[4,320,180]{2,1,0:T(8,128)S(1)} %add.27, f32[4,320,180]{2,1,0:T(8,128)} %copy.35) | non-fusion elementwise | flops 230400 | bytes 2764800 | tf_op jit(solution)/shard_map/add | solution.py:49
  109.7 2.4 copy.36
  112.2 2.5 %collective-permute-start.2 = (f32[4,320,180]{1,0,2:T(4,128)}, f32[4,320,180]{1,0,2:T(4,128)}, u32[]{:S(2)}, u32[]{:S(2)}) collective-permute-start(f32[4,320,180]{1,0,2:T(4,128)} %copy.36), channel_id=1, source_target_pairs={{0,16},{4,20},{8,24},{12,28},{16,0},{20,4},{24,8},{28,12},{1,17},{... | collective-permute-start | bytes 2764808 | tf_op jit(solution)/shard_map/ppermute | solution.py:46
  115.9 45.6 %collective-permute-done.2 = f32[4,320,180]{1,0,2:T(4,128)} collective-permute-done((f32[4,320,180]{1,0,2:T(4,128)}, f32[4,320,180]{1,0,2:T(4,128)}, u32[]{:S(2)}, u32[]{:S(2)}) %collective-permute-start.2) | collective-permute-done | bytes 921632 | tf_op jit(solution)/shard_map/ppermute | solution.py:46
  161.5 2.3 constant_dynamic-slice_fusion
  165.8 1.2 fusion.22
  167.1 2.6 %fusion = f32[32,40,180]{2,1,0:T(8,128)S(1)} fusion(bf16[32,4,40,180]{3,2,1,0:T(8,128)(2,1)} %param.17, f32[4,40,180]{2,1,0:T(8,128)S(1)} %fusion.22), kind=kLoop, calls=%fused_computation.2 | loop fusion | flops 2534400 | bytes 2880000 | tf_op jit(solution)/shard_map/reduce_sum | solution.py:63
  170.0 1.5 copy-done.1
  172.2 31.6 %all_gather.3 = bf16[4,320,180]{2,0,1:T(4,128)(2,1)S(1)} all-gather(bf16[4,40,180]{2,0,1:T(4,128)(2,1)S(1)} %copy.40), channel_id=1, replica_groups=mesh['mem'=8,'band'=4] {'mem'}, dimensions={1}, use_global_device_ids=true | all-gather | bytes 518400 | tf_op jit(solution)/shard_map/all_gather | solution.py:65
  207.0 2.5 %fusion.6 = bf16[3,4,320,180]{2,3,1,0:T(8,128)(2,1)} fusion(bf16[1,4,320,180]{2,3,1,0:T(8,128)(2,1)S(1)} %fusion.19, bf16[2,4,320,180]{2,3,1,0:T(8,128)(2,1)S(1)} %multiply_convert_fusion, bf16[320,320]{1,0:T(8,128)(2,1)S(1)} %copy-done.10), kind=kOutput, calls=%fused_computation.14 | convolution fusion | flops 443750400 | bytes 2969600 | tf_op jit(solution)/shard_map/ji,msjk->msik/dot_general | solution.py:71
  209.5 6.7 %copy.43 = bf16[3,4,320,180]{3,1,0,2:T(4,128)(2,1)S(1)} copy(bf16[3,4,320,180]{2,3,1,0:T(8,128)(2,1)} %fusion.6) | data formatting | bytes 2764800 | tf_op jit(solution)/shard_map/convert_element_type | solution.py:73
  216.2 26.8 %all_to_all.33 = bf16[3,4,320,180]{3,1,0,2:T(4,128)(2,1)S(1)} all-to-all(bf16[3,4,320,180]{3,1,0,2:T(4,128)(2,1)S(1)} %copy.43), channel_id=1, replica_groups=mesh['mem'=8,'band'=4] {'band'}, dimensions={2} | all-to-all | bytes 2764800 | tf_op jit(solution)/shard_map/all_to_all | solution.py:74
  244.3 2.5 all_to_all.30
  246.9 2.8 %fusion.15 = f32[3,4,80,720]{3,2,1,0:T(8,128)S(1)} fusion(bf16[3,4,80,720]{3,2,1,0:T(8,128)(2,1)} %all_to_all.30, bf16[720,720]{1,0:T(8,128)(2,1)S(1)} %copy-done), kind=kOutput, calls=%fused_computation.24 | convolution fusion | flops 995328000 | bytes 5184000 | tf_op jit(solution)/shard_map/msil,jl->msij/dot_general | solution.py:75
  251.2 1.5 slice_add_fusion
  (43 shorter events, 12.3 us)
Async XLA Ops:
  0.6 1.3 copy-start
  7.8 4.4 %copy-start.11 = (s32[16]{0:T(128)S(1)}, s32[16]{0:T(128)}, u32[]{:S(2)}) copy-start(s32[16]{0:T(128)} %param.21) | copy-start | bytes 196
  7.8 31.3 %all-to-all-start = ((bf16[3,4,80,720]{2,1,0,3:T(4,128)(2,1)}), bf16[3,4,80,720]{2,1,0,3:T(4,128)(2,1)S(1)}, u32[]{:S(2)}, u32[]{:S(2)}) async-start(bf16[3,4,80,720]{2,1,0,3:T(4,128)(2,1)} %copy.28), calls=%async_computation | async-start | bytes 4423680 | tf_op jit(solution)/shard_map/all_to_all | solution.py:29
  42.8 1.6 copy-start.4
  42.8 1.7 copy-start.9
  47.2 26.6 %collective-permute-start = (f32[4,320,180]{1,0,2:T(4,128)}, f32[4,320,180]{1,0,2:T(4,128)S(1)}, u32[]{:S(2)}, u32[]{:S(2)}) collective-permute-start(f32[4,320,180]{1,0,2:T(4,128)} %copy.31), channel_id=1, source_target_pairs={{0,4},{4,0},{8,12},{12,8},{16,20},{20,16},{24,28},{28,24},{1,5},{5... | collective-permute-start | bytes 2764808 | tf_op jit(solution)/shard_map/ppermute | solution.py:46
  79.4 25.5 %collective-permute-start.1 = (f32[4,320,180]{1,0,2:T(4,128)}, f32[4,320,180]{1,0,2:T(4,128)S(1)}, u32[]{:S(2)}, u32[]{:S(2)}) collective-permute-start(f32[4,320,180]{1,0,2:T(4,128)} %copy.34), channel_id=1, source_target_pairs={{0,8},{4,12},{8,0},{12,4},{16,24},{20,28},{24,16},{28,20},{1,9},{5... | collective-permute-start | bytes 2764808 | tf_op jit(solution)/shard_map/ppermute | solution.py:46
  109.7 5.0 %copy-start.12 = (f32[32]{0:T(128)S(1)}, f32[32]{0:T(128)}, u32[]{:S(2)}) copy-start(f32[32]{0:T(128)} %param.20) | copy-start | bytes 388
  109.7 5.0 %copy-start.8 = (s32[40,180]{1,0:T(8,128)S(1)}, s32[40,180]{1,0:T(8,128)}, u32[]{:S(2)}) copy-start(s32[40,180]{1,0:T(8,128)} %param.18) | copy-start | bytes 86404
  109.7 51.8 %copy-start.2 = (f32[4,320,180]{1,0,2:T(4,128)S(1)}, f32[4,320,180]{1,0,2:T(4,128)}, u32[]{:S(2)}) copy-start(f32[4,320,180]{1,0,2:T(4,128)} %param.14) | copy-start | bytes 2764804
  112.2 49.3 %collective-permute-start.2 = (f32[4,320,180]{1,0,2:T(4,128)}, f32[4,320,180]{1,0,2:T(4,128)}, u32[]{:S(2)}, u32[]{:S(2)}) collective-permute-start(f32[4,320,180]{1,0,2:T(4,128)} %copy.36), channel_id=1, source_target_pairs={{0,16},{4,20},{8,24},{12,28},{16,0},{20,4},{24,8},{28,12},{1,17},{... | collective-permute-start | bytes 2764808 | tf_op jit(solution)/shard_map/ppermute | solution.py:46
  167.0 2.7 %copy-start.3 = (s32[32,40,180]{2,1,0:T(8,128)S(1)}, s32[32,40,180]{2,1,0:T(8,128)}, u32[]{:S(2)}) copy-start(s32[32,40,180]{2,1,0:T(8,128)} %param.19) | copy-start | bytes 2764804
  169.7 1.7 copy-start.1
  204.8 1.2 copy-start.5
  206.1 0.9 copy-start.10
  246.9 2.8 %copy-start.7 = (bf16[4,80,720]{2,1,0:T(8,128)(2,1)S(1)}, bf16[4,80,720]{2,1,0:T(8,128)(2,1)}, u32[]{:S(2)}) copy-start(bf16[4,80,720]{2,1,0:T(8,128)(2,1)} %param.12) | copy-start | bytes 1382404
  249.7 1.6 copy-start.6
